TPU v7x, 32 devices: a whole 2x2x4 slice. The times are simulated.
32 devices in a mesh: replica: 8 (over z, core), group: 4 (over y, x).
Axes of the slice: x: 2, y: 2, z: 4, core: 2. Of those that a mesh axis runs over, the one named last changes fastest.
Arguments:
- tokens: bfloat16 [4096, 2048], P(('replica', 'group')), may hold values from -6 to 6
- lengths: int32 [8], P('replica'), may hold values from 128 to 512, as said below
- exit_layers: int32 [4096], P(('replica', 'group')), may hold values from 7 to 20, as said below
- pre_gain: bfloat16 [2048], P('group'), may hold values from 0.099609375 to 1.8984375
- pre_shift: bfloat16 [2048], P('group'), may hold values from -3 to 3
- query_weight: bfloat16 [2048, 2048], P('group'), may hold values from -0.1875 to 0.1875
- query_bias: bfloat16 [2048], P('group'), may hold values from -3 to 3
- key_weight: bfloat16 [2048, 2048], P('group'), may hold values from -0.1875 to 0.1875
- value_weight: bfloat16 [2048, 2048], P('group'), may hold values from -0.125 to 0.125
- value_bias: bfloat16 [2048], P('group'), may hold values from -3 to 3
- out_weight: bfloat16 [2048, 2048], P('group'), may hold values from -0.5 to 0.5
- out_bias: bfloat16 [2048], P('group'), may hold values from -1.75 to 1.75
- mid_gain: bfloat16 [2048], P('group'), may hold values from 0.099609375 to 1.8984375
- mid_shift: bfloat16 [2048], P('group'), may hold values from -3 to 3
- up_weight: bfloat16 [2048, 8192], P(None, 'group'), may hold values from -0.125 to 0.125
- up_bias: bfloat16 [8192], P('group'), may hold values from -3 to 3
- down_weight: bfloat16 [8192, 2048], P('group'), may hold values from -0.0625 to 0.0625
- down_bias: bfloat16 [2048], P('group'), may hold values from -1.75 to 1.75
- cotangent: bfloat16 [4096, 2048], P(('replica', 'group')), may hold values from -6 to 6
Outputs:
- output: bfloat16 [4096, 2048], P(('replica', 'group'))
- token_grad: bfloat16 [4096, 2048], P(('replica', 'group'))
- pre_gain_grad: float32 [2048], P('group')
- pre_shift_grad: float32 [2048], P('group')
- query_weight_grad: float32 [2048, 2048], P('group')
- query_bias_grad: float32 [2048], P('group')
- key_weight_grad: float32 [2048, 2048], P('group')
- value_weight_grad: float32 [2048, 2048], P('group')
- value_bias_grad: float32 [2048], P('group')
- out_weight_grad: float32 [2048, 2048], P('group')
- out_bias_grad: float32 [2048], P('group')
- mid_gain_grad: float32 [2048], P('group')
- mid_shift_grad: float32 [2048], P('group')
- up_weight_grad: float32 [2048, 8192], P(None, 'group')
- up_bias_grad: float32 [8192], P('group')
- down_weight_grad: float32 [8192, 2048], P('group')
- down_bias_grad: float32 [2048], P('group')
Inputs may be any that keep to these rules, and one draw needn't show every extreme that they name: `lengths`: some sequence has length 512 and some other has length 128. Within each sequence, exit_layers never rise from one position to the next.
All inputs are finite; a program needn't handle non-finite values.
Results may differ from a plain program's by a relative error of at most 0.02.
Values may be sent and summed in bfloat16 or wider, within the bound.
No kernel may reach another device: no remote copies, remote signals or barrier semaphores. Data moves between devices by JAX's collectives and lax.ppermute only.
A program may use at most 640 MiB of HBM per device.

v0:
```python
import jax
import jax.numpy as jnp
from jax import lax
from jax.sharding import PartitionSpec as P

D = 2048
H = 32
HD = 64
LAYER = 12


def layer_norm(values):
    center = values - jnp.mean(values, -1, keepdims=True)
    spread = jnp.mean(center * center, -1, keepdims=True)
    factor = lax.rsqrt(spread + 1e-05)
    return (center * factor, factor)


def norm_back(grad, normal, factor):
    return factor * (
        grad
        - jnp.mean(grad, -1, keepdims=True)
        - normal * jnp.mean(grad * normal, -1, keepdims=True)
    )


def gelu(values):
    return (
        0.5
        * values
        * (1.0 + jnp.tanh(0.7978845608 * (values + 0.044715 * values * values * values)))
    )


def gelu_back(values, grad):
    inner = 0.7978845608 * (values + 0.044715 * values * values * values)
    tangent = jnp.tanh(inner)
    slope = 0.5 * (1.0 + tangent) + 0.5 * values * (1.0 - tangent * tangent) * 0.7978845608 * (
        1.0 + 3.0 * 0.044715 * values * values
    )
    return grad * slope


def split_heads(matrix):
    groups = max(1, H // 8)
    return matrix.reshape(matrix.shape[0], groups, H // groups, HD).transpose(1, 0, 2, 3)


def join_heads(heads):
    return heads.transpose(1, 0, 2, 3).reshape(heads.shape[1], D)


def score_block(query_group, key_group, allowed):
    scores = (
        jnp.einsum("qhd,khd->hqk", query_group, key_group, preferred_element_type=jnp.float32)
        * 0.125
    )
    return jnp.where(allowed[None], scores, -1e30)


def matmul(left, right):
    return jnp.dot(left, right, preferred_element_type=jnp.float32)


def column_sums(matrix):
    return jnp.sum(matrix.astype(jnp.float32), 0)


def shards(
    tokens,
    lengths,
    exit_layers,
    pre_gain,
    pre_shift,
    query_weight,
    query_bias,
    key_weight,
    value_weight,
    value_bias,
    out_weight,
    out_bias,
    mid_gain,
    mid_shift,
    up_weight,
    up_bias,
    down_weight,
    down_bias,
    cotangent,
):
    local_rows = tokens.shape[0]
    group_count = lax.axis_size("group")
    seq_rows = local_rows * group_count
    member = lax.axis_index("group")
    position = member * local_rows + jnp.arange(local_rows, dtype=jnp.int32)
    active = ((position < lengths[0]) & (exit_layers > LAYER)).astype(jnp.float32)[:, None]
    allowed = jnp.arange(seq_rows, dtype=jnp.int32)[None, :] <= position[:, None]
    (
        gain_one,
        shift_one,
        gain_two,
        shift_two,
        query_full,
        key_full,
        value_full,
        out_full,
        qbias_full,
        vbias_full,
        obias_full,
    ) = (
        lax.all_gather(pre_gain, "group", axis=0, tiled=True),
        lax.all_gather(pre_shift, "group", axis=0, tiled=True),
        lax.all_gather(mid_gain, "group", axis=0, tiled=True),
        lax.all_gather(mid_shift, "group", axis=0, tiled=True),
        lax.all_gather(query_weight, "group", axis=0, tiled=True),
        lax.all_gather(key_weight, "group", axis=0, tiled=True),
        lax.all_gather(value_weight, "group", axis=0, tiled=True),
        lax.all_gather(out_weight, "group", axis=0, tiled=True),
        lax.all_gather(query_bias, "group", axis=0, tiled=True),
        lax.all_gather(value_bias, "group", axis=0, tiled=True),
        lax.all_gather(out_bias, "group", axis=0, tiled=True),
    )
    inputs = tokens.astype(jnp.float32)
    normed_one, factor_one = layer_norm(inputs)
    attn_in = (normed_one * gain_one.astype(jnp.float32) + shift_one.astype(jnp.float32)).astype(
        jnp.bfloat16
    )
    queries = (matmul(attn_in, query_full) + qbias_full.astype(jnp.float32)).astype(jnp.bfloat16)
    keys_local = matmul(attn_in, key_full).astype(jnp.bfloat16)
    values_local = (matmul(attn_in, value_full) + vbias_full.astype(jnp.float32)).astype(
        jnp.bfloat16
    )
    keys_all, values_all = (
        lax.all_gather(keys_local, "group", axis=0, tiled=True),
        lax.all_gather(values_local, "group", axis=0, tiled=True),
    )
    query_heads = split_heads(queries)
    key_heads = split_heads(keys_all)
    value_heads = split_heads(values_all)

    def forward_group(operands):
        query_group, key_group, value_group = operands
        scores = score_block(query_group, key_group, allowed)
        top = jnp.max(scores, -1, keepdims=True)
        logsum = top + jnp.log(jnp.sum(jnp.exp(scores - top), -1, keepdims=True))
        weights = jnp.exp(scores - logsum).astype(jnp.bfloat16)
        context_part = jnp.einsum(
            "hqk,khd->qhd", weights, value_group, preferred_element_type=jnp.float32
        )
        return (context_part, logsum[..., 0])

    context_heads, logsums = lax.map(forward_group, (query_heads, key_heads, value_heads))
    context_low = join_heads(context_heads).astype(jnp.bfloat16)
    attn_out = matmul(context_low, out_full) + obias_full.astype(jnp.float32)
    hidden = inputs + active * attn_out
    normed_two, factor_two = layer_norm(hidden)
    ffn_in = (normed_two * gain_two.astype(jnp.float32) + shift_two.astype(jnp.float32)).astype(
        jnp.bfloat16
    )
    up_full, upbias_full, down_full, downbias_full = (
        lax.all_gather(up_weight, "group", axis=1, tiled=True),
        lax.all_gather(up_bias, "group", axis=0, tiled=True),
        lax.all_gather(down_weight, "group", axis=0, tiled=True),
        lax.all_gather(down_bias, "group", axis=0, tiled=True),
    )
    pre_act = matmul(ffn_in, up_full) + upbias_full.astype(jnp.float32)
    act_low = gelu(pre_act).astype(jnp.bfloat16)
    branch = matmul(act_low, down_full) + downbias_full.astype(jnp.float32)
    output = (hidden + active * branch).astype(jnp.bfloat16)
    first_gain, second_gain, query_back, key_back, value_back, out_back = (
        lax.all_gather(pre_gain, "group", axis=0, tiled=True),
        lax.all_gather(mid_gain, "group", axis=0, tiled=True),
        lax.all_gather(query_weight, "group", axis=0, tiled=True),
        lax.all_gather(key_weight, "group", axis=0, tiled=True),
        lax.all_gather(value_weight, "group", axis=0, tiled=True),
        lax.all_gather(out_weight, "group", axis=0, tiled=True),
    )
    grad_out = cotangent.astype(jnp.float32)
    branch_grad = (active * grad_out).astype(jnp.bfloat16)
    up_back, down_back = (
        lax.all_gather(up_weight, "group", axis=1, tiled=True),
        lax.all_gather(down_weight, "group", axis=0, tiled=True),
    )
    act_grad = matmul(branch_grad, down_back.T)
    pre_grad = gelu_back(pre_act, act_grad).astype(jnp.bfloat16)
    ffn_in_grad = matmul(pre_grad, up_back.T)
    up_grad, up_bias_grad, down_grad, down_bias_grad = (
        lax.psum_scatter(
            matmul(ffn_in.T, pre_grad).astype(jnp.bfloat16),
            "group",
            scatter_dimension=1,
            tiled=True,
        ).astype(jnp.float32),
        lax.psum_scatter(
            column_sums(pre_grad).astype(jnp.bfloat16), "group", scatter_dimension=0, tiled=True
        ).astype(jnp.float32),
        lax.psum_scatter(
            matmul(act_low.T, branch_grad).astype(jnp.bfloat16),
            "group",
            scatter_dimension=0,
            tiled=True,
        ).astype(jnp.float32),
        lax.psum_scatter(
            column_sums(branch_grad).astype(jnp.bfloat16), "group", scatter_dimension=0, tiled=True
        ).astype(jnp.float32),
    )
    mid_gain_part = jnp.sum(ffn_in_grad * normed_two, 0)
    mid_shift_part = jnp.sum(ffn_in_grad, 0)
    hidden_grad = grad_out + norm_back(
        ffn_in_grad * second_gain.astype(jnp.float32), normed_two, factor_two
    )
    attn_grad = (active * hidden_grad).astype(jnp.bfloat16)
    context_grad = matmul(attn_grad, out_back.T).astype(jnp.bfloat16)
    out_bias_part = column_sums(attn_grad)

    def backward_group(operands):
        query_group, key_group, value_group, grad_group, logsum_group = operands
        scores = score_block(query_group, key_group, allowed)
        probs = jnp.exp(scores - logsum_group[..., None])
        probs_grad = jnp.einsum(
            "qhd,khd->hqk", grad_group, value_group, preferred_element_type=jnp.float32
        )
        delta = jnp.sum(probs * probs_grad, -1, keepdims=True)
        score_grad = (probs * (probs_grad - delta)).astype(jnp.bfloat16)
        query_part = (
            jnp.einsum("hqk,khd->qhd", score_grad, key_group, preferred_element_type=jnp.float32)
            * 0.125
        )
        key_part = (
            jnp.einsum("hqk,qhd->khd", score_grad, query_group, preferred_element_type=jnp.float32)
            * 0.125
        )
        value_part = jnp.einsum(
            "hqk,qhd->khd",
            probs.astype(jnp.bfloat16),
            grad_group,
            preferred_element_type=jnp.float32,
        )
        return (query_part, key_part, value_part)

    query_parts, key_parts, value_parts = lax.map(
        backward_group, (query_heads, key_heads, value_heads, split_heads(context_grad), logsums)
    )
    query_grad = join_heads(query_parts).astype(jnp.bfloat16)
    key_sum, value_sum = (
        lax.psum_scatter(
            join_heads(key_parts).astype(jnp.bfloat16), "group", scatter_dimension=0, tiled=True
        ).astype(jnp.float32),
        lax.psum_scatter(
            join_heads(value_parts).astype(jnp.bfloat16), "group", scatter_dimension=0, tiled=True
        ).astype(jnp.float32),
    )
    key_grad = key_sum.astype(jnp.bfloat16)
    value_grad = value_sum.astype(jnp.bfloat16)
    in_grad = (
        matmul(query_grad, query_back.T)
        + matmul(key_grad, key_back.T)
        + matmul(value_grad, value_back.T)
    )
    pre_gain_part = jnp.sum(in_grad * normed_one, 0)
    pre_shift_part = jnp.sum(in_grad, 0)
    token_grad = (
        hidden_grad + norm_back(in_grad * first_gain.astype(jnp.float32), normed_one, factor_one)
    ).astype(jnp.bfloat16)
    (
        pre_gain_grad,
        pre_shift_grad,
        mid_gain_grad,
        mid_shift_grad,
        query_wgrad,
        key_wgrad,
        value_wgrad,
        out_wgrad,
        query_bgrad,
        value_bgrad,
        out_bgrad,
    ) = (
        lax.psum_scatter(
            pre_gain_part.astype(jnp.bfloat16), "group", scatter_dimension=0, tiled=True
        ).astype(jnp.float32),
        lax.psum_scatter(
            pre_shift_part.astype(jnp.bfloat16), "group", scatter_dimension=0, tiled=True
        ).astype(jnp.float32),
        lax.psum_scatter(
            mid_gain_part.astype(jnp.bfloat16), "group", scatter_dimension=0, tiled=True
        ).astype(jnp.float32),
        lax.psum_scatter(
            mid_shift_part.astype(jnp.bfloat16), "group", scatter_dimension=0, tiled=True
        ).astype(jnp.float32),
        lax.psum_scatter(
            matmul(attn_in.T, query_grad).astype(jnp.bfloat16),
            "group",
            scatter_dimension=0,
            tiled=True,
        ).astype(jnp.float32),
        lax.psum_scatter(
            matmul(attn_in.T, key_grad).astype(jnp.bfloat16),
            "group",
            scatter_dimension=0,
            tiled=True,
        ).astype(jnp.float32),
        lax.psum_scatter(
            matmul(attn_in.T, value_grad).astype(jnp.bfloat16),
            "group",
            scatter_dimension=0,
            tiled=True,
        ).astype(jnp.float32),
        lax.psum_scatter(
            matmul(context_low.T, attn_grad).astype(jnp.bfloat16),
            "group",
            scatter_dimension=0,
            tiled=True,
        ).astype(jnp.float32),
        lax.psum_scatter(
            column_sums(query_grad).astype(jnp.bfloat16), "group", scatter_dimension=0, tiled=True
        ).astype(jnp.float32),
        lax.psum_scatter(
            column_sums(value_grad).astype(jnp.bfloat16), "group", scatter_dimension=0, tiled=True
        ).astype(jnp.float32),
        lax.psum_scatter(
            out_bias_part.astype(jnp.bfloat16), "group", scatter_dimension=0, tiled=True
        ).astype(jnp.float32),
    )
    totals = (
        lax.psum(pre_gain_grad.astype(jnp.bfloat16), "replica").astype(jnp.float32),
        lax.psum(pre_shift_grad.astype(jnp.bfloat16), "replica").astype(jnp.float32),
        lax.psum(query_wgrad.astype(jnp.bfloat16), "replica").astype(jnp.float32),
        lax.psum(query_bgrad.astype(jnp.bfloat16), "replica").astype(jnp.float32),
        lax.psum(key_wgrad.astype(jnp.bfloat16), "replica").astype(jnp.float32),
        lax.psum(value_wgrad.astype(jnp.bfloat16), "replica").astype(jnp.float32),
        lax.psum(value_bgrad.astype(jnp.bfloat16), "replica").astype(jnp.float32),
        lax.psum(out_wgrad.astype(jnp.bfloat16), "replica").astype(jnp.float32),
        lax.psum(out_bgrad.astype(jnp.bfloat16), "replica").astype(jnp.float32),
        lax.psum(mid_gain_grad.astype(jnp.bfloat16), "replica").astype(jnp.float32),
        lax.psum(mid_shift_grad.astype(jnp.bfloat16), "replica").astype(jnp.float32),
        lax.psum(up_grad.astype(jnp.bfloat16), "replica").astype(jnp.float32),
        lax.psum(up_bias_grad.astype(jnp.bfloat16), "replica").astype(jnp.float32),
        lax.psum(down_grad.astype(jnp.bfloat16), "replica").astype(jnp.float32),
        lax.psum(down_bias_grad.astype(jnp.bfloat16), "replica").astype(jnp.float32),
    )
    return (
        output,
        token_grad,
        totals[0],
        totals[1],
        totals[2],
        totals[3],
        totals[4],
        totals[5],
        totals[6],
        totals[7],
        totals[8],
        totals[9],
        totals[10],
        totals[11],
        totals[12],
        totals[13],
        totals[14],
    )


def solution(mesh):
    return jax.shard_map(
        shards,
        mesh=mesh,
        in_specs=(
            P(("replica", "group"), None),
            P("replica"),
            P(("replica", "group")),
            P("group"),
            P("group"),
            P("group", None),
            P("group"),
            P("group", None),
            P("group", None),
            P("group"),
            P("group", None),
            P("group"),
            P("group"),
            P("group"),
            P(None, "group"),
            P("group"),
            P("group", None),
            P("group"),
            P(("replica", "group"), None),
        ),
        out_specs=(
            P(("replica", "group"), None),
            P(("replica", "group"), None),
            P("group"),
            P("group"),
            P("group", None),
            P("group"),
            P("group", None),
            P("group", None),
            P("group"),
            P("group", None),
            P("group"),
            P("group"),
            P("group"),
            P(None, "group"),
            P("group"),
            P("group", None),
            P("group"),
        ),
        check_vma=False,
    )
```

profile of v0, /device:TPU:0, one launch (start us, length us, event | category | flops | bytes accessed | tf_op | source)
XLA Modules:
  0.0 2687.4 jit_solution(7998907598796842740)
XLA Ops:
  9.5 9.5 all-gather.2
  19.1 8.1 all-gather.1
  27.2 7.1 all-gather
  34.8 65.6 %all-gather.17.cloned.1.call-done = bf16[2048,2048]{1,0:T(8,128)(2,1)} async-done(((bf16[512,2048]{1,0:T(8,128)(2,1)}), bf16[2048,2048]{1,0:T(8,128)(2,1)}) %all-gather.17.cloned.1.call-update) | async-done | bytes 8388624 | tf_op jit(solution)/shard_map/all_gather | solution.py:116
  100.3 5.5 fusion.50
  105.9 83.9 %all-gather.23.cloned.1.call-done = bf16[2048,2048]{1,0:T(8,128)(2,1)} async-done(((bf16[512,2048]{1,0:T(8,128)(2,1)}), bf16[2048,2048]{1,0:T(8,128)(2,1)}) %all-gather.23.cloned.1.call-update) | async-done | bytes 8388624 | tf_op jit(solution)/shard_map/all_gather | solution.py:115
  189.8 5.5 convolution_convert_fusion.7
  197.6 8.0 all-gather.4
  205.7 7.1 all-gather.3
  213.5 8.3 all_gather.73
  221.8 7.1 all-gather.6
  229.0 8.0 all-gather.5
  237.1 42.5 %all-gather.21.cloned.1.call-done = bf16[2048,2048]{1,0:T(8,128)(2,1)} async-done(((bf16[512,2048]{1,0:T(8,128)(2,1)}), bf16[2048,2048]{1,0:T(8,128)(2,1)}) %all-gather.21.cloned.1.call-update) | async-done | bytes 8388624 | tf_op jit(solution)/shard_map/all_gather | solution.py:114
  279.6 4.7 fusion.51
  284.6 32.6 %all-gather.19.cloned.1.call-done = bf16[512,2048]{1,0:T(8,128)(2,1)} async-done(((bf16[128,2048]{1,0:T(8,128)(2,1)}), bf16[512,2048]{1,0:T(8,128)(2,1)}) %all-gather.19.cloned.1.call-update) | async-done | bytes 2097168 | tf_op jit(solution)/shard_map/all_gather | solution.py:134
  317.2 4.1 copy.44
  321.3 33.5 %all-gather.25.cloned.1.call-done = bf16[512,2048]{1,0:T(8,128)(2,1)} async-done(((bf16[128,2048]{1,0:T(8,128)(2,1)}), bf16[512,2048]{1,0:T(8,128)(2,1)}) %all-gather.25.cloned.1.call-update) | async-done | bytes 2097168 | tf_op jit(solution)/shard_map/all_gather | solution.py:133
  354.8 2.9 copy.46
  358.6 15.8 while.28
  360.0 1.7 fusion.126
  363.9 1.8 fusion.126
  368.0 1.7 fusion.126
  371.9 1.7 fusion.126
  374.4 69.8 %all-gather.27.cloned.1.call-done = bf16[2048,2048]{1,0:T(8,128)(2,1)} async-done(((bf16[512,2048]{1,0:T(8,128)(2,1)}), bf16[2048,2048]{1,0:T(8,128)(2,1)}) %all-gather.27.cloned.1.call-update) | async-done | bytes 8388624 | tf_op jit(solution)/shard_map/all_gather | solution.py:117
  444.1 5.0 fusion.80
  450.3 292.9 %all-gather.29.cloned.1.call-done = bf16[2048,8192]{1,0:T(8,128)(2,1)} async-done(((bf16[2048,2048]{1,0:T(8,128)(2,1)}), bf16[2048,8192]{1,0:T(8,128)(2,1)}) %all-gather.29.cloned.1.call-update) | async-done | bytes 33554448 | tf_op jit(solution)/shard_map/all_gather | solution.py:160
  743.3 20.8 convolution_add_fusion
  764.0 278.3 %all-gather.31.cloned.1.call-done = bf16[8192,2048]{1,0:T(8,128)(2,1)} async-done(((bf16[2048,2048]{1,0:T(8,128)(2,1)}), bf16[8192,2048]{1,0:T(8,128)(2,1)}) %all-gather.31.cloned.1.call-update) | async-done | bytes 33554448 | tf_op jit(solution)/shard_map/all_gather | solution.py:162
  1042.3 18.8 fusion.81
  1061.2 19.7 multiply_reduce_fusion.1
  1080.8 3.3 fusion.78
  1085.0 7.1 convolution_convert_fusion.6
  1092.0 2.0 copy.47
  1095.0 31.3 %while.29 = (s32[]{:T(128)}, bf16[4,128,8,64]{1,3,2,0:T(8,128)(2,1)}, bf16[4,512,8,64]{1,3,2,0:T(8,128)(2,1)}, bf16[4,512,8,64]{1,3,2,0:T(8,128)(2,1)}, bf16[4,5...) while((s32[]{:T(128)}, ...), condition=%wide.region_12.13_spmd.clone, body=%wide.region_10.12_spmd.clone.sunk | while | flops 340655104 | bytes 58091296 | solution.py:240
  1126.3 3.9 copy.48
  1130.2 4.0 copy.50
  1134.3 5.9 convolution_convert_fusion.5
  1141.4 5.5 convolution_convert_fusion.2
  1147.0 18.6 reduce-scatter.25.cloned.1.call-done
  1165.6 6.9 convolution_convert_fusion.4
  1172.5 31.9 %reduce-scatter.27.cloned.1.call-done = bf16[128,2048]{1,0:T(8,128)(2,1)} async-done(((bf16[512,2048]{1,0:T(8,128)(2,1)}), bf16[128,2048]{1,0:T(8,128)(2,1)}) %reduce-scatter.27.cloned.1.call-update) | async-done | bytes 524304
  1204.4 6.8 convolution_convert_fusion.3
  1212.4 15.7 convolution_convert_fusion
  1229.1 16.6 convolution_convert_fusion.1
  1245.8 48.8 %reduce-scatter.15.cloned.1.call-done = bf16[512,2048]{1,0:T(8,128)(2,1)} async-done(((bf16[2048,2048]{1,0:T(8,128)(2,1)}), bf16[512,2048]{1,0:T(8,128)(2,1)}) %reduce-scatter.15.cloned.1.call-update) | async-done | bytes 2097168 | tf_op jit(solution)/shard_map/reduce_scatter | solution.py:289
  1294.5 89.6 %reduce-scatter.21.cloned.1.call-done = bf16[512,2048]{1,0:T(8,128)(2,1)} async-done(((bf16[2048,2048]{1,0:T(8,128)(2,1)}), bf16[512,2048]{1,0:T(8,128)(2,1)}) %reduce-scatter.21.cloned.1.call-update) | async-done | bytes 2097168 | tf_op jit(solution)/shard_map/reduce_scatter | solution.py:307
  1384.2 90.1 %reduce-scatter.17.cloned.1.call-done = bf16[512,2048]{1,0:T(8,128)(2,1)} async-done(((bf16[2048,2048]{1,0:T(8,128)(2,1)}), bf16[512,2048]{1,0:T(8,128)(2,1)}) %reduce-scatter.17.cloned.1.call-update) | async-done | bytes 2097168 | tf_op jit(solution)/shard_map/reduce_scatter | solution.py:295
  1474.2 89.6 %reduce-scatter.19.cloned.1.call-done = bf16[512,2048]{1,0:T(8,128)(2,1)} async-done(((bf16[2048,2048]{1,0:T(8,128)(2,1)}), bf16[512,2048]{1,0:T(8,128)(2,1)}) %reduce-scatter.19.cloned.1.call-update) | async-done | bytes 2097168 | tf_op jit(solution)/shard_map/reduce_scatter | solution.py:301
  1563.9 291.6 %reduce-scatter.23.cloned.1.call-done = bf16[2048,2048]{1,0:T(8,128)(2,1)} async-done(((bf16[2048,8192]{1,0:T(8,128)(2,1)}), bf16[2048,2048]{1,0:T(8,128)(2,1)}) %reduce-scatter.23.cloned.1.call-update) | async-done | bytes 8388624 | tf_op jit(solution)/shard_map/reduce_scatter | solution.py:187
  1855.5 291.9 %reduce-scatter.29.cloned.1.call-done = bf16[2048,2048]{1,0:T(8,128)(2,1)} async-done(((bf16[8192,2048]{1,0:T(8,128)(2,1)}), bf16[2048,2048]{1,0:T(8,128)(2,1)}) %reduce-scatter.29.cloned.1.call-update) | async-done | bytes 8388624
  2148.0 8.1 all-gather.7
  2158.5 6.3 fusion.82
  2164.9 18.0 fusion.52
  2183.0 6.5 convolution_add_fusion.3
  2189.5 6.8 fusion.66
  2196.2 16.3 all-reduce.12
  2213.1 28.0 %all-reduce.10 = (bf16[512]{0:T(512)(128)(2,1)S(1)}, bf16[512]{0:T(512)(128)(2,1)S(1)}, bf16[512]{0:T(512)(128)(2,1)S(1)}, bf16[512]{0:T(512)(128)(2,1)S(1)}, bf...) all-reduce(bf16[512]{0:T(512)(128)(2,1)S(1)} %dynamic-slice.1, ...), channel_id=1, replica_groups=mesh['replica'=8,'group'=4] {'replica'}, use_global_device_ids=true, to_apply=%region_19.20 | all-reduce | flops 6144 | bytes 24576 | tf_op jit(solution)/shard_map/psum | solution.py:324
  2247.6 397.6 %all-reduce.15.cloned.1.call-done = (bf16[512,2048]{1,0:T(8,128)(2,1)}, bf16[512,2048]{1,0:T(8,128)(2,1)}, bf16[512,2048]{1,0:T(8,128)(2,1)}, bf16[512,2048]{1,0...) async-done(((bf16[512,2048]{1,0:T(8,128)(2,1)}, bf16[512,2048]{1,0:T(8,128)(2,1)}, bf16[512,2048]{1,0:T(8,128)(2,1)}, bf16[512,2048]{1,0:T(8,128)(2,1)}, ...) | async-done | bytes 25165840 | tf_op jit(solution)/shard_map/psum | solution.py:326
  2645.2 4.3 convert_element_type.281
  2649.5 2.5 convert_element_type.284
  2652.0 2.5 convert_element_type.286
  2654.6 2.5 convert_element_type.289
  2657.1 11.7 convert_element_type.296
  2668.8 11.7 convert_element_type.299
  (252 shorter events, 61.3 us)
Async XLA Ops:
  7.2 2.3 copy-start.22
  7.2 11.9 copy-start.23
  7.2 19.9 copy-start.24
  7.2 27.1 %copy-start = (bf16[128,2048]{1,0:T(8,128)(2,1)S(1)}, bf16[128,2048]{1,0:T(8,128)(2,1)}, u32[]{:S(2)}) copy-start(bf16[128,2048]{1,0:T(8,128)(2,1)} %param.23) | copy-start | bytes 1572868
  7.2 93.1 %all-gather.17.cloned.1.call-start = ((), (), s32[]{:S(2)}) async-start(), calls=%async_computation.8 | async-start | bytes 10485760 | tf_op jit(solution)/shard_map/all_gather | solution.py:116
  8.0 181.9 %all-gather.23.cloned.1.call-start = ((), (), s32[]{:S(2)}) async-start(), calls=%async_computation.11 | async-start | bytes 10485760 | tf_op jit(solution)/shard_map/all_gather | solution.py:115
  8.7 270.9 %all-gather.21.cloned.1.call-start = ((), (), s32[]{:S(2)}) async-start(), calls=%async_computation.10 | async-start | bytes 10485760 | tf_op jit(solution)/shard_map/all_gather | solution.py:114
  9.4 307.7 %all-gather.19.cloned.1.call-start = ((), (), s32[]{:S(2)}) async-start(), calls=%async_computation.9 | async-start | bytes 2621440 | tf_op jit(solution)/shard_map/all_gather | solution.py:134
  105.9 248.9 %all-gather.25.cloned.1.call-start = ((), (), s32[]{:S(2)}) async-start(), calls=%async_computation.12 | async-start | bytes 2621440 | tf_op jit(solution)/shard_map/all_gather | solution.py:133
  195.4 248.8 %all-gather.27.cloned.1.call-start = ((), (), s32[]{:S(2)}) async-start(), calls=%async_computation.13 | async-start | bytes 10485760 | tf_op jit(solution)/shard_map/all_gather | solution.py:117
  195.9 547.3 %all-gather.29.cloned.1.call-start = ((), (), s32[]{:S(2)}) async-start(), calls=%async_computation.14 | async-start | bytes 41943040 | tf_op jit(solution)/shard_map/all_gather | solution.py:160
  196.7 9.0 copy-start.26
  196.7 16.8 copy-start.21
  196.7 25.1 copy-start.27
  196.7 32.2 %copy-start.28 = (bf16[512]{0:T(512)(128)(2,1)S(1)}, bf16[512]{0:T(512)(128)(2,1)}, u32[]{:S(2)}) copy-start(bf16[512]{0:T(512)(128)(2,1)} %param.35) | copy-start | bytes 3076
  196.7 40.3 %copy-start.30 = (s32[128]{0:T(128)S(1)}, s32[128]{0:T(128)}, u32[]{:S(2)}) copy-start(s32[128]{0:T(128)} %param.25) | copy-start | bytes 1540
  196.8 845.6 %all-gather.31.cloned.1.call-start = ((), (), s32[]{:S(2)}) async-start(), calls=%async_computation.15 | async-start | bytes 41943040 | tf_op jit(solution)/shard_map/all_gather | solution.py:162
  197.5 968.0 %reduce-scatter.25.cloned.1.call-start = ((), (), s32[]{:S(2)}) async-start(), calls=%async_computation.21 | async-start | bytes 2621440
  358.6 1.4 copy-start.3
  362.5 1.4 copy-start.3
  366.5 1.4 copy-start.3
  370.5 1.4 copy-start.3
  1096.7 1.2 copy-start.6
  1097.7 1.6 copy-start.17
  1097.7 2.4 copy-start.19
  1098.5 3.0 copy-start.7
  1099.6 1.9 copy-start.18
  1101.5 1.3 copy-start.20
  1104.6 1.2 copy-start.6
  1105.5 1.6 copy-start.17
  1105.5 2.4 copy-start.19
  1106.3 3.0 copy-start.7
  1107.4 1.9 copy-start.18
  1109.3 1.3 copy-start.20
  1112.4 1.2 copy-start.6
  1113.3 1.6 copy-start.17
  1113.3 2.4 copy-start.19
  1114.1 3.0 copy-start.7
  1115.2 1.9 copy-start.18
  1117.1 1.3 copy-start.20
  1120.2 1.2 copy-start.6
  1121.1 1.6 copy-start.17
  1121.2 2.4 copy-start.19
  1121.9 3.0 copy-start.7
  1123.1 1.9 copy-start.18
  1124.9 1.3 copy-start.20
  1130.2 4.1 copy-start.8
  1130.2 74.2 %reduce-scatter.27.cloned.1.call-start = ((), (), s32[]{:S(2)}) async-start(), calls=%async_computation.22 | async-start | bytes 2621440
  1134.2 160.3 %reduce-scatter.15.cloned.1.call-start = ((), (), s32[]{:S(2)}) async-start(), calls=%async_computation.16 | async-start | bytes 10485760 | tf_op jit(solution)/shard_map/reduce_scatter | solution.py:289
  1140.2 1.0 copy-start.5
  1140.2 1.2 copy-start.11
  1140.2 244.0 %reduce-scatter.21.cloned.1.call-start = ((), (), s32[]{:S(2)}) async-start(), calls=%async_computation.19 | async-start | bytes 10485760 | tf_op jit(solution)/shard_map/reduce_scatter | solution.py:307
  1146.9 327.3 %reduce-scatter.17.cloned.1.call-start = ((), (), s32[]{:S(2)}) async-start(), calls=%async_computation.17 | async-start | bytes 10485760 | tf_op jit(solution)/shard_map/reduce_scatter | solution.py:295
  1172.5 391.4 %reduce-scatter.19.cloned.1.call-start = ((), (), s32[]{:S(2)}) async-start(), calls=%async_computation.18 | async-start | bytes 10485760 | tf_op jit(solution)/shard_map/reduce_scatter | solution.py:301
  1211.2 1.2 copy-start.2
  1211.2 644.3 %reduce-scatter.23.cloned.1.call-start = ((), (), s32[]{:S(2)}) async-start(), calls=%async_computation.20 | async-start | bytes 41943040 | tf_op jit(solution)/shard_map/reduce_scatter | solution.py:187
  1228.1 919.2 %reduce-scatter.29.cloned.1.call-start = ((), (), s32[]{:S(2)}) async-start(), calls=%async_computation.23 | async-start | bytes 41943040
  1245.7 1399.5 %all-reduce.15.cloned.1.call-start = ((), (), s32[]{:S(2)}) async-start(), calls=%async_computation.24 | async-start | bytes 50331648 | tf_op jit(solution)/shard_map/psum | solution.py:326
  2147.4 8.8 copy-start.31
  2164.8 18.1 copy-start.9
  2189.5 56.9 %copy-start.12 = (f32[128,2048]{1,0:T(8,128)S(1)}, f32[128,2048]{1,0:T(8,128)}, u32[]{:S(2)}) copy-start(f32[128,2048]{1,0:T(8,128)} %get-tuple-element.224) | copy-start | bytes 3145732
  2645.2 4.3 copy-start.16
  2649.5 2.5 copy-start.15
  2652.0 2.5 copy-start.14
  (9 other events, 7.6 us)
Sparse Core Ops, SparseCore 0:
  9.9 90.3 all-gather.16
  102.2 87.5 all-gather.22
  191.7 87.8 all-gather.20
  281.8 35.3 all-gather.18
  319.5 35.2 all-gather.24
  356.5 87.5 all-gather.26
  446.0 297.2 all-gather.28
  745.1 297.2 all-gather.30
  1130.3 35.1 reduce-scatter.24
  1169.2 35.1 reduce-scatter.26
  1208.1 86.3 reduce-scatter.14
  1297.7 86.3 reduce-scatter.20
  1387.8 86.3 reduce-scatter.16
  1477.4 86.3 reduce-scatter.18
  1566.8 288.6 reduce-scatter.22
  1858.7 288.6 reduce-scatter.28
  2150.5 494.6 all-reduce.14
where the time goes:
time: 2690 us
  waiting for transfers between devices  2250 us (84%)
  matrix products  210 us (8%)
  blocking collectives  116 us (4%)
  other arithmetic  50.9 us (2%)
  local copies, waits for them, and re-layouts  39.5 us (1%)
    psum x1, waiting for transfers between devices, shards(): lax.psum(query_wgrad.astype(jnp.bfloat16), 'replica').astype(jnp.float32)  398 us
    unnamed x20, waiting for transfers between devices  346 us
    all_gather x1, waiting for transfers between devices, shards(): lax.all_gather(up_weight, 'group', axis=1, tiled=True)  293 us
    reduce_scatter x1, waiting for transfers between devices, shards(): lax.psum_scatter(matmul(ffn_in.T, pre_grad).astype(jnp.bfloat16), 'group'...  292 us
    all_gather x1, waiting for transfers between devices, shards(): lax.all_gather(down_weight, 'group', axis=0, tiled=True)  278 us
    dot_general x18, matrix products, matmul(): return jnp.dot(left, right, preferred_element_type=jnp.float32)  182 us
    reduce_scatter x1, waiting for transfers between devices, shards(): lax.psum_scatter(matmul(attn_in.T, key_grad).astype(jnp.bfloat16), 'group...  90.1 us
    reduce_scatter x1, waiting for transfers between devices, shards(): lax.psum_scatter(matmul(attn_in.T, value_grad).astype(jnp.bfloat16), 'gro...  89.6 us
  transfers between devices with their start and end apart: 17, of which 17 were waited for; matrix products, arithmetic and copies ran while one was open for 6% of the time, Pallas kernels for 0%

commit v1 on v0

--- a/solution.py
+++ b/solution.py
@@ -7,6 +7,13 @@
 H = 32
 HD = 64
 LAYER = 12
+
+
+def swapped_in(x, name, along):
+    peers = lax.axis_size(name)
+    pieces = jnp.stack([x for _ in range(peers)])
+    pieces = lax.all_to_all(pieces, name, split_axis=0, concat_axis=0)
+    return jnp.concatenate(pieces, axis=along)
 
 
 def layer_norm(values):
@@ -114,7 +121,7 @@
         lax.all_gather(query_weight, "group", axis=0, tiled=True),
         lax.all_gather(key_weight, "group", axis=0, tiled=True),
         lax.all_gather(value_weight, "group", axis=0, tiled=True),
-        lax.all_gather(out_weight, "group", axis=0, tiled=True),
+        swapped_in(out_weight, "group", 0),
         lax.all_gather(query_bias, "group", axis=0, tiled=True),
         lax.all_gather(value_bias, "group", axis=0, tiled=True),
         lax.all_gather(out_bias, "group", axis=0, tiled=True),

time: 2690 us -> 2730 us (1.015)
  blocking collectives: 116 us -> 240 us
  waiting for transfers between devices: 2250 us -> 2150 us
    all_gather x1, blocking collectives: 8.03 us -> 132 us  [shards(): lax.all_gather(out_bias, 'group', axis=0, tiled=True)]
    all_gather x1, waiting for transfers between devices: 42.5 us -> 0.02 us  [shards(): lax.all_gather(query_weight, 'group', axis=0, tiled=True)]
  transfers between devices with their start and end apart: 17 -> 18, of which waited for: 17 -> 16; matrix products, arithmetic and copies ran while one was open for 6% -> 8% of each run, Pallas kernels for 0% -> 0%
where the time goes in v1:
time: 2730 us
  waiting for transfers between devices  2150 us (79%)
  blocking collectives  240 us (9%)
  matrix products  214 us (8%)
  other arithmetic  51 us (2%)
  local copies, waits for them, and re-layouts  44.9 us (2%)
    psum x1, waiting for transfers between devices, shards(): lax.psum(query_wgrad.astype(jnp.bfloat16), 'replica').astype(jnp.float32)  398 us
    unnamed x20, waiting for transfers between devices  347 us
    reduce_scatter x1, waiting for transfers between devices, shards(): lax.psum_scatter(matmul(ffn_in.T, pre_grad).astype(jnp.bfloat16), 'group'...  292 us
    all_gather x1, waiting for transfers between devices, shards(): lax.all_gather(down_weight, 'group', axis=0, tiled=True)  278 us
    all_gather x1, waiting for transfers between devices, shards(): lax.all_gather(up_weight, 'group', axis=1, tiled=True)  271 us
    dot_general x18, matrix products, matmul(): return jnp.dot(left, right, preferred_element_type=jnp.float32)  186 us
    all_gather x1, blocking collectives, shards(): lax.all_gather(out_bias, 'group', axis=0, tiled=True)  132 us
    reduce_scatter x1, waiting for transfers between devices, shards(): lax.psum_scatter(matmul(attn_in.T, key_grad).astype(jnp.bfloat16), 'group...  90 us
  transfers between devices with their start and end apart: 18, of which 16 were waited for; matrix products, arithmetic and copies ran while one was open for 8% of the time, Pallas kernels for 0%

profile of v1, /device:TPU:0, one launch (start us, length us, event | category | flops | bytes accessed | tf_op | source)
XLA Modules:
  0.0 2727.3 jit_solution(519952414104864720)
XLA Ops:
  9.5 9.5 all-gather.2
  19.1 8.1 all-gather.1
  27.2 7.1 all-gather
  34.8 65.6 %all-gather.17.cloned.1.call-done = bf16[2048,2048]{1,0:T(8,128)(2,1)} async-done(((bf16[512,2048]{1,0:T(8,128)(2,1)}), bf16[2048,2048]{1,0:T(8,128)(2,1)}) %all-gather.17.cloned.1.call-update) | async-done | bytes 8388624 | tf_op jit(solution)/shard_map/all_gather | solution.py:123
  100.3 5.5 fusion.50
  105.9 83.9 %all-gather.23.cloned.1.call-done = bf16[2048,2048]{1,0:T(8,128)(2,1)} async-done(((bf16[512,2048]{1,0:T(8,128)(2,1)}), bf16[2048,2048]{1,0:T(8,128)(2,1)}) %all-gather.23.cloned.1.call-update) | async-done | bytes 8388624 | tf_op jit(solution)/shard_map/all_gather | solution.py:122
  189.8 5.5 convolution_convert_fusion.7
  197.5 5.3 stack.2
  202.8 5.8 all-to-all-start
  209.5 132.0 %all-gather.4 = bf16[4,1,512]{2,1,0:T(2,128)(2,1)S(1)} all-gather(bf16[1,1,512]{2,1,0:T(2,128)(2,1)S(1)} %reshape.159), channel_id=1, replica_groups=mesh['replica'=8,'group'=4] {'group'}, dimensions={0}, use_global_device_ids=true | all-gather | bytes 5120 | tf_op jit(solution)/shard_map/all_gather | solution.py:127
  341.5 8.1 all-gather.3
  350.3 7.3 all_gather.71
  357.7 8.1 all-gather.6
  365.8 7.0 all-gather.5
  372.9 4.7 fusion.51
  377.9 21.5 all-gather.19.cloned.1.call-done
  399.4 4.1 copy.44
  403.6 33.5 %all-gather.25.cloned.1.call-done = bf16[512,2048]{1,0:T(8,128)(2,1)} async-done(((bf16[128,2048]{1,0:T(8,128)(2,1)}), bf16[512,2048]{1,0:T(8,128)(2,1)}) %all-gather.25.cloned.1.call-update) | async-done | bytes 2097168 | tf_op jit(solution)/shard_map/all_gather | solution.py:140
  437.1 2.9 copy.46
  440.8 16.0 while.28
  446.2 1.9 fusion.126
  450.3 1.8 fusion.126
  454.3 1.7 fusion.126
  456.9 7.3 fusion.80
  465.4 270.6 %all-gather.27.cloned.1.call-done = bf16[2048,8192]{1,0:T(8,128)(2,1)} async-done(((bf16[2048,2048]{1,0:T(8,128)(2,1)}), bf16[2048,8192]{1,0:T(8,128)(2,1)}) %all-gather.27.cloned.1.call-update) | async-done | bytes 33554448 | tf_op jit(solution)/shard_map/all_gather | solution.py:167
  736.0 20.8 convolution_add_fusion
  756.8 278.3 %all-gather.29.cloned.1.call-done = bf16[8192,2048]{1,0:T(8,128)(2,1)} async-done(((bf16[2048,2048]{1,0:T(8,128)(2,1)}), bf16[8192,2048]{1,0:T(8,128)(2,1)}) %all-gather.29.cloned.1.call-update) | async-done | bytes 33554448 | tf_op jit(solution)/shard_map/all_gather | solution.py:169
  1035.1 20.4 fusion.81
  1055.5 19.7 multiply_reduce_fusion.1
  1075.2 3.5 fusion.78
  1078.7 45.9 %all-gather.31.cloned.1.call-done = bf16[2048,2048]{1,0:T(8,128)(2,1)} async-done(((bf16[512,2048]{1,0:T(8,128)(2,1)}), bf16[2048,2048]{1,0:T(8,128)(2,1)}) %all-gather.31.cloned.1.call-update) | async-done | bytes 8388624 | tf_op jit(solution)/shard_map/all_gather | solution.py:182
  1124.6 7.3 convolution_convert_fusion.6
  1131.8 2.1 copy.47
  1134.8 31.3 %while.29 = (s32[]{:T(128)}, bf16[4,128,8,64]{1,3,2,0:T(8,128)(2,1)}, bf16[4,512,8,64]{1,3,2,0:T(8,128)(2,1)}, bf16[4,512,8,64]{1,3,2,0:T(8,128)(2,1)}, bf16[4,5...) while((s32[]{:T(128)}, ...), condition=%wide.region_12.13_spmd.clone, body=%wide.region_10.12_spmd.clone.sunk | while | flops 340655104 | bytes 58091296 | solution.py:247
  1166.1 3.9 copy.48
  1170.1 4.0 copy.50
  1174.1 5.9 convolution_convert_fusion.5
  1181.2 5.6 convolution_convert_fusion.2
  1186.8 18.6 reduce-scatter.25.cloned.1.call-done
  1205.4 6.9 convolution_convert_fusion.4
  1212.4 31.9 %reduce-scatter.27.cloned.1.call-done = bf16[128,2048]{1,0:T(8,128)(2,1)} async-done(((bf16[512,2048]{1,0:T(8,128)(2,1)}), bf16[128,2048]{1,0:T(8,128)(2,1)}) %reduce-scatter.27.cloned.1.call-update) | async-done | bytes 524304
  1244.3 6.8 convolution_convert_fusion.3
  1252.3 15.7 convolution_convert_fusion
  1269.0 16.5 convolution_convert_fusion.1
  1285.6 48.8 %reduce-scatter.15.cloned.1.call-done = bf16[512,2048]{1,0:T(8,128)(2,1)} async-done(((bf16[2048,2048]{1,0:T(8,128)(2,1)}), bf16[512,2048]{1,0:T(8,128)(2,1)}) %reduce-scatter.15.cloned.1.call-update) | async-done | bytes 2097168 | tf_op jit(solution)/shard_map/reduce_scatter | solution.py:296
  1334.3 89.7 %reduce-scatter.21.cloned.1.call-done = bf16[512,2048]{1,0:T(8,128)(2,1)} async-done(((bf16[2048,2048]{1,0:T(8,128)(2,1)}), bf16[512,2048]{1,0:T(8,128)(2,1)}) %reduce-scatter.21.cloned.1.call-update) | async-done | bytes 2097168 | tf_op jit(solution)/shard_map/reduce_scatter | solution.py:314
  1424.0 90.0 %reduce-scatter.17.cloned.1.call-done = bf16[512,2048]{1,0:T(8,128)(2,1)} async-done(((bf16[2048,2048]{1,0:T(8,128)(2,1)}), bf16[512,2048]{1,0:T(8,128)(2,1)}) %reduce-scatter.17.cloned.1.call-update) | async-done | bytes 2097168 | tf_op jit(solution)/shard_map/reduce_scatter | solution.py:302
  1514.0 89.7 %reduce-scatter.19.cloned.1.call-done = bf16[512,2048]{1,0:T(8,128)(2,1)} async-done(((bf16[2048,2048]{1,0:T(8,128)(2,1)}), bf16[512,2048]{1,0:T(8,128)(2,1)}) %reduce-scatter.19.cloned.1.call-update) | async-done | bytes 2097168 | tf_op jit(solution)/shard_map/reduce_scatter | solution.py:308
  1603.7 291.6 %reduce-scatter.23.cloned.1.call-done = bf16[2048,2048]{1,0:T(8,128)(2,1)} async-done(((bf16[2048,8192]{1,0:T(8,128)(2,1)}), bf16[2048,2048]{1,0:T(8,128)(2,1)}) %reduce-scatter.23.cloned.1.call-update) | async-done | bytes 8388624 | tf_op jit(solution)/shard_map/reduce_scatter | solution.py:194
  1895.3 291.9 %reduce-scatter.29.cloned.1.call-done = bf16[2048,2048]{1,0:T(8,128)(2,1)} async-done(((bf16[8192,2048]{1,0:T(8,128)(2,1)}), bf16[2048,2048]{1,0:T(8,128)(2,1)}) %reduce-scatter.29.cloned.1.call-update) | async-done | bytes 8388624
  2187.9 8.1 all-gather.7
  2198.4 6.3 fusion.82
  2204.7 18.0 fusion.52
  2222.8 6.5 convolution_add_fusion.3
  2229.3 6.8 fusion.66
  2236.1 16.2 all-reduce.12
  2253.0 28.0 %all-reduce.10 = (bf16[512]{0:T(512)(128)(2,1)S(1)}, bf16[512]{0:T(512)(128)(2,1)S(1)}, bf16[512]{0:T(512)(128)(2,1)S(1)}, bf16[512]{0:T(512)(128)(2,1)S(1)}, bf...) all-reduce(bf16[512]{0:T(512)(128)(2,1)S(1)} %dynamic-slice.1, ...), channel_id=1, replica_groups=mesh['replica'=8,'group'=4] {'replica'}, use_global_device_ids=true, to_apply=%region_19.20 | all-reduce | flops 6144 | bytes 24576 | tf_op jit(solution)/shard_map/psum | solution.py:331
  2287.5 397.6 %all-reduce.15.cloned.1.call-done = (bf16[512,2048]{1,0:T(8,128)(2,1)}, bf16[512,2048]{1,0:T(8,128)(2,1)}, bf16[512,2048]{1,0:T(8,128)(2,1)}, bf16[512,2048]{1,0...) async-done(((bf16[512,2048]{1,0:T(8,128)(2,1)}, bf16[512,2048]{1,0:T(8,128)(2,1)}, bf16[512,2048]{1,0:T(8,128)(2,1)}, bf16[512,2048]{1,0:T(8,128)(2,1)}, ...) | async-done | bytes 25165840 | tf_op jit(solution)/shard_map/psum | solution.py:333
  2685.1 4.3 convert_element_type.283
  2689.3 2.5 convert_element_type.286
  2691.9 2.5 convert_element_type.288
  2694.4 2.5 convert_element_type.291
  2697.0 11.7 convert_element_type.298
  2708.6 11.7 convert_element_type.301
  (255 shorter events, 63.0 us)
Async XLA Ops:
  7.2 2.3 copy-start.22
  7.2 11.9 copy-start.23
  7.2 19.9 copy-start.24
  7.2 27.1 copy-start
  7.2 93.1 %all-gather.17.cloned.1.call-start = ((), (), s32[]{:S(2)}) async-start(), calls=%async_computation.9 | async-start | bytes 10485760 | tf_op jit(solution)/shard_map/all_gather | solution.py:123
  8.0 181.9 %all-gather.23.cloned.1.call-start = ((), (), s32[]{:S(2)}) async-start(), calls=%async_computation.12 | async-start | bytes 10485760 | tf_op jit(solution)/shard_map/all_gather | solution.py:122
  8.7 364.2 %all-gather.21.cloned.1.call-start = ((), (), s32[]{:S(2)}) async-start(), calls=%async_computation.11 | async-start | bytes 10485760 | tf_op jit(solution)/shard_map/all_gather | solution.py:121
  9.4 390.0 %all-gather.19.cloned.1.call-start = ((), (), s32[]{:S(2)}) async-start(), calls=%async_computation.10 | async-start | bytes 2621440 | tf_op jit(solution)/shard_map/all_gather | solution.py:141
  105.9 331.2 %all-gather.25.cloned.1.call-start = ((), (), s32[]{:S(2)}) async-start(), calls=%async_computation.13 | async-start | bytes 2621440 | tf_op jit(solution)/shard_map/all_gather | solution.py:140
  195.4 540.7 %all-gather.27.cloned.1.call-start = ((), (), s32[]{:S(2)}) async-start(), calls=%async_computation.14 | async-start | bytes 41943040 | tf_op jit(solution)/shard_map/all_gather | solution.py:167
  195.9 1.6 copy-start.6
  195.9 839.2 %all-gather.29.cloned.1.call-start = ((), (), s32[]{:S(2)}) async-start(), calls=%async_computation.15 | async-start | bytes 41943040 | tf_op jit(solution)/shard_map/all_gather | solution.py:169
  202.8 6.6 copy-start.25
  202.8 138.7 %copy-start.26 = (bf16[512]{0:T(512)(128)(2,1)S(1)}, bf16[512]{0:T(512)(128)(2,1)}, u32[]{:S(2)}) copy-start(bf16[512]{0:T(512)(128)(2,1)} %param.29) | copy-start | bytes 3076
  202.8 147.5 %copy-start.21 = (bf16[2048]{0:T(1024)(128)(2,1)S(1)}, bf16[2048]{0:T(1024)(128)(2,1)}, u32[]{:S(2)}) copy-start(bf16[2048]{0:T(1024)(128)(2,1)} %param.38) | copy-start | bytes 12292
  202.8 154.9 %copy-start.27 = (bf16[512]{0:T(512)(128)(2,1)S(1)}, bf16[512]{0:T(512)(128)(2,1)}, u32[]{:S(2)}) copy-start(bf16[512]{0:T(512)(128)(2,1)} %param.36) | copy-start | bytes 3076
  202.8 163.0 %copy-start.28 = (bf16[512]{0:T(512)(128)(2,1)S(1)}, bf16[512]{0:T(512)(128)(2,1)}, u32[]{:S(2)}) copy-start(bf16[512]{0:T(512)(128)(2,1)} %param.35) | copy-start | bytes 3076
  202.8 170.1 %copy-start.30 = (s32[128]{0:T(128)S(1)}, s32[128]{0:T(128)}, u32[]{:S(2)}) copy-start(s32[128]{0:T(128)} %param.25) | copy-start | bytes 1540
  202.8 254.0 %all-to-all-start = ((bf16[4,512,2048]{2,1,0:T(8,128)(2,1)}), bf16[4,512,2048]{2,1,0:T(8,128)(2,1)}, u32[]{:S(2)}, u32[]{:S(2)}) async-start(bf16[4,512,2048]{2,1,0:T(8,128)(2,1)} %stack.2), calls=%async_computation | async-start | bytes 16777216 | tf_op jit(solution)/shard_map/all_to_all | solution.py:15
  208.6 916.0 %all-gather.31.cloned.1.call-start = ((), (), s32[]{:S(2)}) async-start(), calls=%async_computation.16 | async-start | bytes 10485760 | tf_op jit(solution)/shard_map/all_gather | solution.py:182
  209.4 996.0 %reduce-scatter.25.cloned.1.call-start = ((), (), s32[]{:S(2)}) async-start(), calls=%async_computation.22 | async-start | bytes 2621440
  440.8 1.4 copy-start.3
  444.8 1.4 copy-start.3
  448.9 1.4 copy-start.3
  452.9 1.4 copy-start.3
  1136.6 1.2 copy-start.7
  1137.5 1.6 copy-start.17
  1137.5 2.4 copy-start.19
  1138.3 3.0 copy-start.8
  1139.4 1.9 copy-start.18
  1141.3 1.3 copy-start.20
  1144.4 1.2 copy-start.7
  1145.3 1.6 copy-start.17
  1145.3 2.4 copy-start.19
  1146.1 3.0 copy-start.8
  1147.3 1.9 copy-start.18
  1149.1 1.3 copy-start.20
  1152.2 1.2 copy-start.7
  1153.2 1.6 copy-start.17
  1153.2 2.4 copy-start.19
  1154.0 3.0 copy-start.8
  1155.1 1.9 copy-start.18
  1156.9 1.3 copy-start.20
  1160.0 1.2 copy-start.7
  1161.0 1.6 copy-start.17
  1161.0 2.4 copy-start.19
  1161.8 3.0 copy-start.8
  1162.9 1.9 copy-start.18
  1164.8 1.3 copy-start.20
  1170.0 4.1 copy-start.9
  1170.0 74.2 %reduce-scatter.27.cloned.1.call-start = ((), (), s32[]{:S(2)}) async-start(), calls=%async_computation.23 | async-start | bytes 2621440
  1174.1 160.3 %reduce-scatter.15.cloned.1.call-start = ((), (), s32[]{:S(2)}) async-start(), calls=%async_computation.17 | async-start | bytes 10485760 | tf_op jit(solution)/shard_map/reduce_scatter | solution.py:296
  1180.0 244.0 %reduce-scatter.21.cloned.1.call-start = ((), (), s32[]{:S(2)}) async-start(), calls=%async_computation.20 | async-start | bytes 10485760 | tf_op jit(solution)/shard_map/reduce_scatter | solution.py:314
  1186.8 327.3 %reduce-scatter.17.cloned.1.call-start = ((), (), s32[]{:S(2)}) async-start(), calls=%async_computation.18 | async-start | bytes 10485760 | tf_op jit(solution)/shard_map/reduce_scatter | solution.py:302
  1212.3 391.4 %reduce-scatter.19.cloned.1.call-start = ((), (), s32[]{:S(2)}) async-start(), calls=%async_computation.19 | async-start | bytes 10485760 | tf_op jit(solution)/shard_map/reduce_scatter | solution.py:308
  1251.1 644.2 %reduce-scatter.23.cloned.1.call-start = ((), (), s32[]{:S(2)}) async-start(), calls=%async_computation.21 | async-start | bytes 41943040 | tf_op jit(solution)/shard_map/reduce_scatter | solution.py:194
  1268.0 919.2 %reduce-scatter.29.cloned.1.call-start = ((), (), s32[]{:S(2)}) async-start(), calls=%async_computation.24 | async-start | bytes 41943040
  1285.5 1399.5 %all-reduce.15.cloned.1.call-start = ((), (), s32[]{:S(2)}) async-start(), calls=%async_computation.25 | async-start | bytes 50331648 | tf_op jit(solution)/shard_map/psum | solution.py:333
  2187.2 8.8 copy-start.31
  2204.7 18.1 copy-start.10
  2229.3 56.9 %copy-start.12 = (f32[128,2048]{1,0:T(8,128)S(1)}, f32[128,2048]{1,0:T(8,128)}, u32[]{:S(2)}) copy-start(f32[128,2048]{1,0:T(8,128)} %get-tuple-element.224) | copy-start | bytes 3145732
  2685.1 4.3 copy-start.16
  2689.3 2.5 copy-start.15
  2691.9 2.5 copy-start.14
  (10 other events, 9.3 us)
Sparse Core Ops, SparseCore 0:
  9.9 90.3 all-gather.16
  102.2 87.5 all-gather.22
  191.7 170.0 all-gather.20
  364.1 35.3 all-gather.18
  401.7 35.2 all-gather.24
  438.8 297.2 all-gather.26
  737.9 297.2 all-gather.28
  1036.9 87.5 all-gather.30
  1170.1 35.1 reduce-scatter.24
  1209.0 35.1 reduce-scatter.26
  1247.9 86.3 reduce-scatter.14
  1337.6 86.4 reduce-scatter.20
  1427.6 86.3 reduce-scatter.16
  1517.3 86.4 reduce-scatter.18
  1606.6 288.6 reduce-scatter.22
  1898.5 288.6 reduce-scatter.28
  2190.3 494.6 all-reduce.14
